TPU v7x, 32 devices: a whole 2x2x4 slice. The times are simulated.
32 devices in a mesh: batch: 8 (over z, y), head: 4 (over x, core).
Axes of the slice: x: 2, y: 2, z: 4, core: 2. Of those that a mesh axis runs over, the one named last changes fastest.
Arguments:
- tokens: bfloat16 [16384, 768], P(('batch', 'head')), may hold values from -6 to 6
- cotangent: bfloat16 [16384, 768], P(('batch', 'head')), may hold values from -6 to 6
- lengths: int32 [32], P('batch'), may hold values from 16 to 512, as said below
- labels: int32 [32], P('batch'), may hold values from 0 to 2
- w_qkv: bfloat16 [768, 2304], replicated, may hold values from -0.21875 to 0.21875
- w_out: bfloat16 [768, 768], replicated, may hold values from -0.875 to 0.875
- w_up: bfloat16 [768, 3072], replicated, may hold values from -0.21875 to 0.21875
- w_down: bfloat16 [3072, 768], replicated, may hold values from -0.109375 to 0.109375
- w_pool: bfloat16 [768, 768], replicated, may hold values from -0.21875 to 0.21875
- w_class: bfloat16 [3, 768], replicated, may hold values from -0.625 to 0.625
- biases: float32 [7, 768], replicated, may hold values from -3 to 3
- norm_gains: float32 [2, 768], replicated, may hold values from 0.25 to 1.75
- bias_up: float32 [3072], replicated, may hold values from -3 to 3
Outputs:
- out: bfloat16 [16384, 768], P(('batch', 'head'))
- grad_tokens: bfloat16 [16384, 768], P(('batch', 'head'))
- losses: float32 [32], P(('batch', 'head'))
- g_qkv: float32 [768, 2304], P(None, ('batch', 'head'))
- g_out: float32 [768, 768], P(None, ('batch', 'head'))
- g_up: float32 [768, 3072], P(None, ('batch', 'head'))
- g_down: float32 [3072, 768], P(None, ('batch', 'head'))
- g_pool: float32 [768, 768], P(None, ('batch', 'head'))
- g_class: float32 [3, 768], P(None, ('batch', 'head'))
- g_biases: float32 [6, 768], P(None, ('batch', 'head'))
- g_gains: float32 [2, 768], P(None, ('batch', 'head'))
- g_bias_up: float32 [3072], P(('batch', 'head'))
- g_pool_bias: float32 [768], P(('batch', 'head'))
Inputs may be any that keep to these rules, and one draw needn't show every extreme that they name: `lengths`: some sequence has exactly 512 and some exactly 16 positions.
All inputs are finite; a program needn't handle non-finite values.
Results may differ from a plain program's by a relative error of at most 0.014.
Values may be sent and summed in bfloat16 or wider, within the bound.
A program may use at most 192 MiB of HBM per device.

v0:
```python
import jax
import jax.numpy as jnp
from jax import lax
from jax.sharding import PartitionSpec as P

D = 768
HEADS = 12
HEAD_DIM = 64
CLASSES = 3
SLOT = 512


def layer_norm(hidden, gain, shift):
    center = hidden - jnp.mean(hidden, axis=-1, keepdims=True)
    spread = jnp.mean(center * center, axis=-1, keepdims=True)
    return center * lax.rsqrt(spread + 1e-12) * gain + shift


def exact_gelu(hidden):
    return jax.nn.gelu(hidden, approximate=False)


def inner(left, right):
    return lax.dot_general(
        left, right, (((0,), (0,)), ((), ())), preferred_element_type=jnp.float32
    )


def against(left, right):
    return lax.dot_general(
        left, right, (((1,), (1,)), ((), ())), preferred_element_type=jnp.float32
    )


def exact(left, right):
    return jnp.dot(left, right, precision=lax.Precision.HIGHEST, preferred_element_type=jnp.float32)


def masked_scores(queries, keys_all, length):
    scores = jnp.einsum(
        "qhd,khd->hqk", queries, keys_all, preferred_element_type=jnp.float32
    ) * HEAD_DIM ** (-0.5)
    allowed = jnp.arange(SLOT) < length
    return jnp.where(allowed[None, None, :], scores, -1e30)


def attend_forward(seq_item):
    packed, length = seq_item
    queries = packed[:, 0]
    keys_all = packed[:, 1]
    values = packed[:, 2]
    scores = masked_scores(queries, keys_all, length)
    row_max = jnp.max(scores, axis=-1, keepdims=True)
    exp_sum = jnp.sum(jnp.exp(scores - row_max), axis=-1, keepdims=True)
    log_total = row_max + jnp.log(exp_sum)
    weights = jnp.exp(scores - log_total).astype(jnp.bfloat16)
    context = jnp.einsum("hqk,khd->qhd", weights, values, preferred_element_type=jnp.float32)
    return (context.astype(jnp.bfloat16), log_total)


def attend_backward(seq_item):
    packed, log_total, d_context, length = seq_item
    queries = packed[:, 0]
    keys_all = packed[:, 1]
    values = packed[:, 2]
    scores = masked_scores(queries, keys_all, length)
    weights = jnp.exp(scores - log_total)
    weights_low = weights.astype(jnp.bfloat16)
    d_weights = jnp.einsum("qhd,khd->hqk", d_context, values, preferred_element_type=jnp.float32)
    d_values = jnp.einsum(
        "hqk,qhd->khd", weights_low, d_context, preferred_element_type=jnp.float32
    )
    row_dot = jnp.sum(weights * d_weights, axis=-1, keepdims=True)
    d_scores = (weights * (d_weights - row_dot)).astype(jnp.bfloat16)
    d_queries = jnp.einsum(
        "hqk,khd->qhd", d_scores, keys_all, preferred_element_type=jnp.float32
    ) * HEAD_DIM ** (-0.5)
    d_keys = jnp.einsum(
        "hqk,qhd->khd", d_scores, queries, preferred_element_type=jnp.float32
    ) * HEAD_DIM ** (-0.5)
    return jnp.stack([d_queries, d_keys, d_values], axis=1).astype(jnp.bfloat16)


def per_device(
    tokens,
    cotangent,
    lengths,
    labels,
    w_qkv,
    w_out,
    w_up,
    w_down,
    w_pool,
    w_class,
    biases,
    norm_gains,
    bias_up,
):
    head_parts = lax.axis_size("head")
    head_rank = lax.axis_index("head")
    tok_rows = tokens.shape[0]
    own_seqs = tok_rows // SLOT
    local_heads = HEADS // head_parts
    slice_width = D // head_parts
    own_lengths = lax.dynamic_slice_in_dim(lengths, head_rank * own_seqs, own_seqs)
    own_labels = lax.dynamic_slice_in_dim(labels, head_rank * own_seqs, own_seqs)
    slot_live = (
        (jnp.arange(SLOT)[None, :] < own_lengths[:, None]).reshape(tok_rows).astype(jnp.float32)
    )
    zeros_key = jnp.zeros((D,), jnp.float32)
    packed = jnp.dot(tokens, w_qkv, preferred_element_type=jnp.float32) + jnp.concatenate(
        [biases[0], zeros_key, biases[1]]
    )
    packed_low = packed.astype(jnp.bfloat16)
    head_view = lax.all_to_all(
        packed_low.reshape(tok_rows, 3, head_parts, slice_width),
        "head",
        split_axis=2,
        concat_axis=0,
        tiled=True,
    )
    seq_view = head_view.reshape(head_parts * own_seqs, SLOT, 3, local_heads, HEAD_DIM)
    context, log_total = lax.map(attend_forward, (seq_view, lengths))
    context_back = lax.all_to_all(
        context.reshape(head_parts * tok_rows, 1, slice_width),
        "head",
        split_axis=0,
        concat_axis=1,
        tiled=True,
    )
    context_tok = context_back.reshape(tok_rows, D)
    attn = jnp.dot(context_tok, w_out, preferred_element_type=jnp.float32) + biases[2]
    first_sum = tokens.astype(jnp.float32) + attn
    norm_one, first_pull = jax.vjp(layer_norm, first_sum, norm_gains[0], biases[3])
    norm_low = norm_one.astype(jnp.bfloat16)
    hidden_up = jnp.dot(norm_low, w_up, preferred_element_type=jnp.float32) + bias_up
    activated_full, gelu_pull = jax.vjp(exact_gelu, hidden_up)
    activated = activated_full.astype(jnp.bfloat16)
    branch = jnp.dot(activated, w_down, preferred_element_type=jnp.float32) + biases[4]
    out_full, second_pull = jax.vjp(layer_norm, norm_one + branch, norm_gains[1], biases[5])
    leading = out_full.reshape(own_seqs, SLOT, D)[:, 0].astype(jnp.bfloat16)
    pooled = jnp.tanh(jnp.dot(leading, w_pool, preferred_element_type=jnp.float32) + biases[6])
    pooled_low = pooled.astype(jnp.bfloat16)
    logits = against(pooled_low, w_class)
    onehot = (jnp.arange(CLASSES)[None, :] == own_labels[:, None]).astype(jnp.float32)
    losses = jax.nn.logsumexp(logits, axis=-1) - jnp.sum(onehot * logits, axis=-1)
    d_logits = jax.nn.softmax(logits, axis=-1) - onehot
    g_class = exact(d_logits.T, pooled_low.astype(jnp.float32))
    d_pre = exact(d_logits, w_class.astype(jnp.float32)) * (1.0 - pooled * pooled)
    g_pool = exact(leading.astype(jnp.float32).T, d_pre)
    g_pool_bias = jnp.sum(d_pre, axis=0)
    d_leading = exact(d_pre, w_pool.astype(jnp.float32).T)
    d_out = cotangent.astype(jnp.float32) * slot_live[:, None]
    d_out = d_out.reshape(own_seqs, SLOT, D).at[:, 0].add(d_leading).reshape(tok_rows, D)
    d_h2, g_gain_two, g_shift_two = second_pull(d_out)
    d_branch = d_h2.astype(jnp.bfloat16)
    g_bias_down = jnp.sum(d_branch.astype(jnp.float32), axis=0)
    g_down = inner(activated, d_branch)
    d_activated = against(d_branch, w_down)
    d_up = gelu_pull(d_activated)[0].astype(jnp.bfloat16)
    g_bias_up = jnp.sum(d_up.astype(jnp.float32), axis=0)
    g_up = inner(norm_low, d_up)
    d_norm_one = d_h2 + against(d_up, w_up)
    d_h1, g_gain_one, g_shift_one = first_pull(d_norm_one)
    d_attn = d_h1.astype(jnp.bfloat16)
    g_bias_out = jnp.sum(d_attn.astype(jnp.float32), axis=0)
    g_out = inner(context_tok, d_attn)
    d_context = against(d_attn, w_out).astype(jnp.bfloat16)
    d_context_heads = lax.all_to_all(
        d_context.reshape(tok_rows, head_parts, slice_width),
        "head",
        split_axis=1,
        concat_axis=0,
        tiled=True,
    )
    d_context_seq = d_context_heads.reshape(head_parts * own_seqs, SLOT, local_heads, HEAD_DIM)
    d_seq = lax.map(attend_backward, (seq_view, log_total, d_context_seq, lengths))
    d_back = lax.all_to_all(
        d_seq.reshape(head_parts * tok_rows, 3, 1, slice_width),
        "head",
        split_axis=0,
        concat_axis=2,
        tiled=True,
    )
    d_packed = d_back.reshape(tok_rows, 3 * D)
    g_qkv = inner(tokens, d_packed)
    column_sums = jnp.sum(d_packed.astype(jnp.float32), axis=0)
    grad_tokens = (d_h1 + against(d_packed, w_qkv)).astype(jnp.bfloat16)
    g_biases = jnp.stack(
        [column_sums[:D], column_sums[2 * D :], g_bias_out, g_shift_one, g_bias_down, g_shift_two]
    )
    g_gains = jnp.stack([g_gain_one, g_gain_two])
    g_qkv, g_out, g_up, g_down, g_pool, g_class, g_biases, g_gains, g_bias_up, g_pool_bias = (
        lax.psum_scatter(g_qkv, ("batch", "head"), scatter_dimension=1, tiled=True),
        lax.psum_scatter(g_out, ("batch", "head"), scatter_dimension=1, tiled=True),
        lax.psum_scatter(g_up, ("batch", "head"), scatter_dimension=1, tiled=True),
        lax.psum_scatter(g_down, ("batch", "head"), scatter_dimension=1, tiled=True),
        lax.psum_scatter(g_pool, ("batch", "head"), scatter_dimension=1, tiled=True),
        lax.psum_scatter(g_class, ("batch", "head"), scatter_dimension=1, tiled=True),
        lax.psum_scatter(g_biases, ("batch", "head"), scatter_dimension=1, tiled=True),
        lax.psum_scatter(g_gains, ("batch", "head"), scatter_dimension=1, tiled=True),
        lax.psum_scatter(g_bias_up, ("batch", "head"), scatter_dimension=0, tiled=True),
        lax.psum_scatter(g_pool_bias, ("batch", "head"), scatter_dimension=0, tiled=True),
    )
    return (
        out_full.astype(jnp.bfloat16),
        grad_tokens,
        losses,
        g_qkv,
        g_out,
        g_up,
        g_down,
        g_pool,
        g_class,
        g_biases,
        g_gains,
        g_bias_up,
        g_pool_bias,
    )


def solution(mesh):
    return jax.shard_map(
        per_device,
        mesh=mesh,
        in_specs=(
            P(("batch", "head"), None),
            P(("batch", "head"), None),
            P("batch"),
            P("batch"),
            P(),
            P(),
            P(),
            P(),
            P(),
            P(),
            P(),
            P(),
            P(),
        ),
        out_specs=(
            P(("batch", "head"), None),
            P(("batch", "head"), None),
            P(("batch", "head")),
            P(None, ("batch", "head")),
            P(None, ("batch", "head")),
            P(None, ("batch", "head")),
            P(None, ("batch", "head")),
            P(None, ("batch", "head")),
            P(None, ("batch", "head")),
            P(None, ("batch", "head")),
            P(None, ("batch", "head")),
            P(("batch", "head")),
            P(("batch", "head")),
        ),
        check_vma=False,
    )
```

profile of v0, /device:TPU:0, one launch (start us, length us, event | category | flops | bytes accessed | tf_op | source)
XLA Modules:
  0.0 791.8 jit_solution(17786111128805935081)
XLA Ops:
  9.3 4.5 fusion.34
  13.8 4.3 copy.63
  18.1 3.2 copy.64
  21.3 4.7 all-to-all-start
  26.0 29.1 %all-to-all-done = bf16[512,3,4,192]{0,3,1,2:T(8,128)(2,1)} async-done(((bf16[512,3,4,192]{0,3,1,2:T(8,128)(2,1)}), bf16[512,3,4,192]{0,3,1,2:T(8,128)(2,1)}, u32[]{:S(2)}, u32[]{:S(2)}) %all-to-all-start) | async-done | bytes 2359328 | tf_op jit(solution)/shard_map/all_to_all | solution.py:115
  55.1 24.0 %while.23 = (s32[]{:T(128)}, bf16[4,512,3,64]{1,3,2,0:T(8,128)(2,1)}, f32[4,3,512,1]{2,1,3,0:T(4,128)}, bf16[4,512,3,3,64]{1,4,3,2,0:T(8,128)(2,1)}, s32[4]{0:T(128)S(1)}, /*index=5*/s32[]{:T(128)}) while((s32[]{:T(128)}, bf16[4,512,3,64]{1,3,2,0:T(8,128)(2,1)}, f32[4,3,512,1]{2,1,3,0:T(4,128)}, bf16[4,512,3,3,64]{1,4,3,2,0:T(8,128)(2,1)}, ...), condition=%wide.region_3.4_spmd, body=%wide.region_0.3_spmd.sunk | while | flops 210074624 | bytes 11459673 | solution.py:123
  90.3 3.9 reshape.384
  94.3 4.2 all-to-all-start.1
  104.6 5.5 all-to-all-done.1
  110.2 4.1 reshape.385
  114.3 5.7 copy.67
  128.2 19.6 %multiply_convert_fusion.1 = (bf16[512,3072]{1,0:T(8,128)(2,1)S(1)}, f32[512,3072]{1,0:T(8,128)}, f32[512,3072]{1,0:T(8,128)}) fusion(f32[3072]{0:T(1024)S(1)} %copy-done.37, bf16[768,3072]{1,0:T(8,128)(2,1)} %param.25, f32[512,768]{1,0:T(8,128)S(1)} %get-tuple-element.165, f32[768]{0:T(1024)S(1)} %copy-done.32, f32[768]{0:T(1024)S(1)} %get-tuple-element.176, ...), kind=kOutput, calls=%fused_computation.50 | convolution fusion | flops 2521694208 | bytes 22042624 | tf_op jit(solution)/shard_map/dot_general | solution.py:136
  163.2 3.2 multiply_reduce_fusion.1
  172.7 9.5 %convert_reduce_fusion = (f32[3072]{0:T(1024)}, bf16[512,3072]{1,0:T(8,128)(2,1)S(1)}) fusion(f32[512,3072]{1,0:T(8,128)} %get-tuple-element.156, f32[512,3072]{1,0:T(8,128)} %get-tuple-element.166, f32[3072]{0:T(1024)} %param.31, bf16[512,768]{1,0:T(8,128)(2,1)S(1)} %get-tuple-element.148, bf16[3072,768]{1,0:T(8,128)(2,1)} %param.26), kind=kOutput, calls=%fused_computation.48 | convolution fusion | flops 2442654720 | bytes 21258240 | tf_op jit(solution)/shard_map/dot_general | solution.py:30
  182.2 7.3 multiply_reduce_fusion.2
  196.5 4.2 all-to-all-start.2
  200.9 3.6 fusion.60
  204.6 7.8 all-to-all-done.2
  212.4 39.9 %while.24 = (s32[]{:T(128)}, bf16[4,512,3,3,64]{1,4,3,2,0:T(8,128)(2,1)}, bf16[4,512,3,3,64]{1,4,3,2,0:T(8,128)(2,1)}, s32[4]{0:T(128)}, f32[4,3,512,1]{2,1,3,0:...) while((s32[]{:T(128)}, bf16[4,512,3,3,64]{1,4,3,2,0:T(8,128)(2,1)}, ...), condition=%wide.region_16.17_spmd, body=%wide.region_14.16_spmd.sunk | while | flops 512654336 | bytes 27953856 | solution.py:177
  252.3 4.9 copy.70
  257.2 5.9 reshape.346
  263.1 7.0 copy.71
  270.0 53.9 %all_to_all.60 = bf16[2048,3,1,192]{3,1,2,0:T(4,128)(2,1)} all-to-all(bf16[2048,3,1,192]{3,1,2,0:T(4,128)(2,1)} %copy.71), channel_id=1, replica_groups=mesh['batch'=8,'head'=4] {'head'}, dimensions={0} | all-to-all | bytes 4718592 | tf_op jit(solution)/shard_map/all_to_all | solution.py:178
  323.9 7.4 copy.80
  335.0 5.0 convolution_bitcast_fusion
  340.2 8.8 %fusion.48 = f32[768,3072]{0,1:T(8,128)} fusion(bf16[512,3072]{1,0:T(8,128)(2,1)} %copy-done.43, f32[512,768]{1,0:T(8,128)} %copy-done.6, f32[768]{0:T(1024)} %get-tuple-element.107, f32[768]{0:T(1024)S(1)} %copy-done.27, f32[512]{0:T(512)} %copy-done.28, f32[512]{0:T(512)S(1)} %copy-done.17), kind=kOutput, calls=%fused_computation.138 | convolution fusion | flops 2417885184 | bytes 14166016 | tf_op jit(solution)/shard_map/dot_general | solution.py:24
  349.1 8.4 %fusion.61 = f32[3072,768]{0,1:T(8,128)} fusion(bf16[512,3072]{1,0:T(8,128)(2,1)} %copy-done.42, bf16[512,768]{1,0:T(8,128)(2,1)} %copy-done.13), kind=kOutput, calls=%fused_computation.148 | convolution fusion | flops 2415919104 | bytes 13369344 | tf_op jit(solution)/shard_map/dot_general | solution.py:24
  375.8 42.2 %all-reduce.5 = (f32[3,768]{1,0:T(4,128)}, f32[6,768]{1,0:T(8,128)}, f32[2,768]{1,0:T(2,128)}, f32[3072]{0:T(1024)}, f32[768]{0:T(1024)}) all-reduce(f32[3,768]{1,0:T(4,128)S(1)} %broadcast_multiply_fusion.1, f32[6,768]{1,0:T(8,128)} %stack.38, ...), channel_id=7, replica_groups=mesh['batch'=8,'head'=4] {'batch','head'}, use_global_device_ids=true, to_apply=%region_24.25.clone | all-reduce | flops 12288 | bytes 98304
  424.6 5.1 add_convert_fusion.1
  429.7 70.9 %reduce-scatter.9.cloned.1.call-done = f32[768,72]{0,1:T(8,128)} async-done(((f32[768,2304]{0,1:T(8,128)}), f32[768,72]{0,1:T(8,128)}) %reduce-scatter.9.cloned.1.call-update) | async-done | bytes 221200 | tf_op jit(solution)/shard_map/reduce_scatter | solution.py:194
  500.6 142.2 %reduce-scatter.13.cloned.1.call-done = f32[768,96]{0,1:T(8,128)} async-done(((f32[768,3072]{0,1:T(8,128)}), f32[768,96]{0,1:T(8,128)}) %reduce-scatter.13.cloned.1.call-update) | async-done | bytes 294928 | tf_op jit(solution)/shard_map/reduce_scatter | solution.py:196
  642.8 140.9 %reduce-scatter.15.cloned.1.call-done = f32[3072,24]{0,1:T(8,128)} async-done(((f32[3072,768]{0,1:T(8,128)}), f32[3072,24]{0,1:T(8,128)}) %reduce-scatter.15.cloned.1.call-update) | async-done | bytes 294928 | tf_op jit(solution)/shard_map/reduce_scatter | solution.py:197
  (254 shorter events, 146.0 us)
Async XLA Ops:
  8.8 139.0 %copy-start.26 = (f32[768]{0:T(1024)}, f32[768]{0:T(1024)S(1)}, u32[]{:S(2)}) copy-start(f32[768]{0:T(1024)S(1)} %get-tuple-element.176) | copy-start | bytes 9220
  21.3 33.8 %copy-start.40 = (s32[4]{0:T(128)S(1)}, s32[4]{0:T(128)}, u32[]{:S(2)}) copy-start(s32[4]{0:T(128)} %param.21) | copy-start | bytes 52
  21.3 33.8 %all-to-all-start = ((bf16[512,3,4,192]{0,3,1,2:T(8,128)(2,1)}), bf16[512,3,4,192]{0,3,1,2:T(8,128)(2,1)}, u32[]{:S(2)}, u32[]{:S(2)}) async-start(bf16[512,3,4,192]{0,3,1,2:T(8,128)(2,1)} %copy.64), calls=%async_computation | async-start | bytes 4718592 | tf_op jit(solution)/shard_map/all_to_all | solution.py:115
  85.1 15.2 %copy-start.39 = (s32[4]{0:T(128)S(1)}, s32[4]{0:T(128)}, u32[]{:S(2)}) copy-start(s32[4]{0:T(128)} %param.22) | copy-start | bytes 52
  94.3 15.9 %all-to-all-start.1 = ((bf16[4,2,49152]{2,1,0:T(2,128)(2,1)}), bf16[4,2,49152]{2,1,0:T(2,128)(2,1)}, u32[]{:S(2)}, u32[]{:S(2)}) async-start(bf16[4,2,49152]{2,1,0:T(2,128)(2,1)} %reshape.384), calls=%async_computation.1 | async-start | bytes 1572864 | tf_op jit(solution)/shard_map/all_to_all | solution.py:124
  98.5 331.2 %reduce-scatter.17.cloned.1.call-start = ((), (), s32[]{:S(2)}) async-start(), calls=%async_computation.13 | async-start | bytes 2433024 | tf_op jit(solution)/shard_map/reduce_scatter | solution.py:198
  114.3 10.0 %copy-start.34 = (f32[768]{0:T(1024)S(1)}, f32[768]{0:T(1024)}, u32[]{:S(2)}) copy-start(f32[768]{0:T(1024)} %get-tuple-element.108) | copy-start | bytes 9220
  124.3 3.9 copy-start.32
  124.4 23.6 %slice-start = ((s8[4718592]{0:T(1024)(128)(4,1)}), s8[4194304]{0:T(1024)(128)(4,1)S(1)}, s32[]{:S(2)}) async-start(s8[4718592]{0:T(1024)(128)(4,1)} %bitcast.202), calls=%async_computation.14 | async-start | bytes 8388608
  127.1 20.8 %copy-start.6 = (f32[512,768]{1,0:T(8,128)}, f32[512,768]{1,0:T(8,128)S(1)}, u32[]{:S(2)}) copy-start(f32[512,768]{1,0:T(8,128)S(1)} %get-tuple-element.165) | copy-start | bytes 4718596
  127.1 20.8 %copy-start.16 = (f32[512]{0:T(512)}, f32[512]{0:T(512)S(1)}, u32[]{:S(2)}) copy-start(f32[512]{0:T(512)S(1)} %broadcast_multiply_fusion.3) | copy-start | bytes 6148
  128.2 19.7 %copy-start.28 = (f32[512]{0:T(512)}, f32[512]{0:T(512)S(1)}, u32[]{:S(2)}) copy-start(f32[512]{0:T(512)S(1)} %fusion.43) | copy-start | bytes 6148
  128.2 19.7 %copy-start.33 = (f32[768]{0:T(1024)S(1)}, f32[768]{0:T(1024)}, u32[]{:S(2)}) copy-start(f32[768]{0:T(1024)} %get-tuple-element.106) | copy-start | bytes 9220
  128.2 19.7 %slice-start.1 = ((s8[4718592]{0:T(1024)(128)(4,1)}), s8[524288]{0:T(1024)(128)(4,1)S(1)}, s32[]{:S(2)}) async-start(s8[4718592]{0:T(1024)(128)(4,1)} %bitcast.202), calls=%async_computation.15 | async-start | bytes 1048576
  150.7 10.5 %copy-start.1 = (f32[512,768]{1,0:T(8,128)}, f32[512,768]{1,0:T(8,128)S(1)}, u32[]{:S(2)}) copy-start(f32[512,768]{1,0:T(8,128)S(1)} %get-tuple-element.168) | copy-start | bytes 4718596
  150.8 10.5 %copy-start.25 = (f32[768]{0:T(1024)S(1)}, f32[768]{0:T(1024)}, u32[]{:S(2)}) copy-start(f32[768]{0:T(1024)} %slice_reduce_fusion) | copy-start | bytes 9220
  163.2 3.9 copy-start.2
  163.2 3.9 copy-start.4
  172.6 9.6 %copy-start.13 = (bf16[512,768]{1,0:T(8,128)(2,1)}, bf16[512,768]{1,0:T(8,128)(2,1)S(1)}, u32[]{:S(2)}) copy-start(bf16[512,768]{1,0:T(8,128)(2,1)S(1)} %get-tuple-element.148) | copy-start | bytes 2359300
  172.6 9.6 %copy-start.7 = (f32[512,768]{1,0:T(8,128)S(1)}, f32[512,768]{1,0:T(8,128)}, u32[]{:S(2)}) copy-start(f32[512,768]{1,0:T(8,128)} %copy-done.6) | copy-start | bytes 4718596
  172.6 9.6 %copy-start.9 = (f32[512,768]{1,0:T(8,128)S(1)}, f32[512,768]{1,0:T(8,128)}, u32[]{:S(2)}) copy-start(f32[512,768]{1,0:T(8,128)} %get-tuple-element.154) | copy-start | bytes 4718596
  172.7 9.6 %copy-start.17 = (f32[512]{0:T(512)S(1)}, f32[512]{0:T(512)}, u32[]{:S(2)}) copy-start(f32[512]{0:T(512)} %copy-done.16) | copy-start | bytes 6148
  172.7 9.5 %copy-start.27 = (f32[768]{0:T(1024)S(1)}, f32[768]{0:T(1024)}, u32[]{:S(2)}) copy-start(f32[768]{0:T(1024)} %copy-done.26) | copy-start | bytes 9220
  172.7 9.5 %copy-start.29 = (f32[512]{0:T(512)S(1)}, f32[512]{0:T(512)}, u32[]{:S(2)}) copy-start(f32[512]{0:T(512)} %copy-done.28) | copy-start | bytes 6148
  182.2 7.3 copy-start.43
  182.2 7.3 copy-start.19
  196.5 15.9 %all-to-all-start.2 = ((bf16[512,4,192]{0,2,1:T(8,128)(2,1)}), bf16[512,4,192]{0,2,1:T(8,128)(2,1)}, u32[]{:S(2)}, u32[]{:S(2)}) async-start(bf16[512,4,192]{0,2,1:T(8,128)(2,1)} %bitcast.198), calls=%async_computation.2 | async-start | bytes 1572864 | tf_op jit(solution)/shard_map/all_to_all | solution.py:169
  200.7 229.0 %reduce-scatter.11.cloned.1.call-start = ((), (), s32[]{:S(2)}) async-start(), calls=%async_computation.10 | async-start | bytes 2433024 | tf_op jit(solution)/shard_map/reduce_scatter | solution.py:195
  204.6 296.0 %reduce-scatter.9.cloned.1.call-start = ((), (), s32[]{:S(2)}) async-start(), calls=%async_computation.9 | async-start | bytes 7299072 | tf_op jit(solution)/shard_map/reduce_scatter | solution.py:194
  339.9 302.9 %reduce-scatter.13.cloned.1.call-start = ((), (), s32[]{:S(2)}) async-start(), calls=%async_computation.11 | async-start | bytes 9732096 | tf_op jit(solution)/shard_map/reduce_scatter | solution.py:196
  349.1 434.6 %reduce-scatter.15.cloned.1.call-start = ((), (), s32[]{:S(2)}) async-start(), calls=%async_computation.12 | async-start | bytes 9732096 | tf_op jit(solution)/shard_map/reduce_scatter | solution.py:197
  358.2 17.6 %copy-start.24 = (f32[768]{0:T(1024)S(1)}, f32[768]{0:T(1024)}, u32[]{:S(2)}) copy-start(f32[768]{0:T(1024)} %get-tuple-element.172) | copy-start | bytes 9220
  (25 other events, 59.5 us)
Sparse Core Ops, SparseCore 0:
  171.1 100.1 reduce-scatter.16
  278.1 98.0 reduce-scatter.10
  382.4 118.0 reduce-scatter.8
  507.9 134.8 reduce-scatter.12
  649.1 134.5 reduce-scatter.14
where the time goes:
time: 800 us; the launch traced here: 792 us
  waiting for transfers between devices  397 us (50%)
  matrix products  112 us (14%)
  local copies, waits for them, and re-layouts  111 us (14%)
  blocking collectives  96.1 us (12%)
  other arithmetic  42.7 us (5%)
  between operations  18.5 us (2%)
  starting transfers between devices  14.2 us (2%)
    reduce_scatter x1, waiting for transfers between devices, per_device(): lax.psum_scatter(g_up, ('batch', 'head'), scatter_dimension=1, tiled=True)  142 us
    reduce_scatter x1, waiting for transfers between devices, per_device(): lax.psum_scatter(g_down, ('batch', 'head'), scatter_dimension=1, tiled=True)  141 us
    reduce_scatter x1, waiting for transfers between devices, per_device(): lax.psum_scatter(g_qkv, ('batch', 'head'), scatter_dimension=1, tiled=True)  70.9 us
    all_to_all x1, blocking collectives, per_device(): lax.all_to_all(d_seq.reshape(head_parts * tok_rows, 3, 1, slice_width), '...  53.9 us
    unnamed x1, blocking collectives  42.2 us
    all_to_all x1, waiting for transfers between devices, per_device(): lax.all_to_all(packed_low.reshape(tok_rows, 3, head_parts, slice_width),...  29.1 us
    dot_general x4, matrix products, inner(): lax.dot_general(left, right, (((0,), (0,)), ((), ())), preferred_element_...  25.8 us
    dot_general x5, matrix products, against(): lax.dot_general(left, right, (((1,), (1,)), ((), ())), preferred_element_...  24.3 us
  transfers between devices with their start and end apart: 8, of which 6 were waited for; matrix products, arithmetic and copies ran while one was open for 19% of the time, Pallas kernels for 0%

commit v1 on v0

--- a/solution.py
+++ b/solution.py
@@ -121,12 +121,20 @@
     )
     seq_view = head_view.reshape(head_parts * own_seqs, SLOT, 3, local_heads, HEAD_DIM)
     context, log_total = lax.map(attend_forward, (seq_view, lengths))
-    context_back = lax.all_to_all(
-        context.reshape(head_parts * tok_rows, 1, slice_width),
-        "head",
-        split_axis=0,
-        concat_axis=1,
-        tiled=True,
+    context_back = jnp.concatenate(
+        lax.all_to_all(
+            jnp.stack(
+                jnp.split(
+                    context.reshape(head_parts * tok_rows, 1, slice_width),
+                    lax.axis_size("head"),
+                    axis=0,
+                )
+            ),
+            "head",
+            0,
+            0,
+        ),
+        axis=1,
     )
     context_tok = context_back.reshape(tok_rows, D)
     attn = jnp.dot(context_tok, w_out, preferred_element_type=jnp.float32) + biases[2]

time: 800 us -> 773 us (0.966)
  local copies, waits for them, and re-layouts: 111 us -> 86.1 us
    unnamed x98 -> x91, local copies, waits for them, and re-layouts: 23.3 us -> 13 us
    all_to_all x3 -> x0, local copies, waits for them, and re-layouts: 9.99 us -> none  [per_device(): lax.all_to_all(context.reshape(head_parts * tok_rows, 1, slice_width), 'h...]
  transfers between devices with their start and end apart: 8 -> 8, of which waited for: 6 -> 6; matrix products, arithmetic and copies ran while one was open for 19% -> 20% of each run, Pallas kernels for 0% -> 0%
where the time goes in v1:
time: 773 us; the launch traced here: 765 us
  waiting for transfers between devices  397 us (51%)
  matrix products  113 us (15%)
  blocking collectives  96.7 us (13%)
  local copies, waits for them, and re-layouts  86.1 us (11%)
  other arithmetic  40.6 us (5%)
  between operations  18.3 us (2%)
  starting transfers between devices  13.2 us (2%)
    reduce_scatter x1, waiting for transfers between devices, per_device(): lax.psum_scatter(g_up, ('batch', 'head'), scatter_dimension=1, tiled=True)  142 us
    reduce_scatter x1, waiting for transfers between devices, per_device(): lax.psum_scatter(g_down, ('batch', 'head'), scatter_dimension=1, tiled=True)  141 us
    reduce_scatter x1, waiting for transfers between devices, per_device(): lax.psum_scatter(g_qkv, ('batch', 'head'), scatter_dimension=1, tiled=True)  70.7 us
    all_to_all x1, blocking collectives, per_device(): lax.all_to_all(d_seq.reshape(head_parts * tok_rows, 3, 1, slice_width), '...  54.1 us
    unnamed x1, blocking collectives  42.6 us
    all_to_all x1, waiting for transfers between devices, per_device(): lax.all_to_all(packed_low.reshape(tok_rows, 3, head_parts, slice_width),...  29.1 us
    dot_general x4, matrix products, inner(): lax.dot_general(left, right, (((0,), (0,)), ((), ())), preferred_element_...  25.8 us
    dot_general x5, matrix products, against(): lax.dot_general(left, right, (((1,), (1,)), ((), ())), preferred_element_...  24.4 us
  transfers between devices with their start and end apart: 8, of which 6 were waited for; matrix products, arithmetic and copies ran while one was open for 20% of the time, Pallas kernels for 0%

profile of v1, /device:TPU:0, one launch (start us, length us, event | category | flops | bytes accessed | tf_op | source)
XLA Modules:
  0.0 765.3 jit_solution(544937717018692600)
XLA Ops:
  9.3 4.5 fusion.34
  13.8 4.3 copy.57
  18.1 3.2 copy.58
  21.3 4.7 all-to-all-start
  26.0 29.1 %all-to-all-done = bf16[512,3,4,192]{0,3,1,2:T(8,128)(2,1)} async-done(((bf16[512,3,4,192]{0,3,1,2:T(8,128)(2,1)}), bf16[512,3,4,192]{0,3,1,2:T(8,128)(2,1)}, u32[]{:S(2)}, u32[]{:S(2)}) %all-to-all-start) | async-done | bytes 2359328 | tf_op jit(solution)/shard_map/all_to_all | solution.py:115
  55.1 24.0 %while.23 = (s32[]{:T(128)}, bf16[4,512,3,64]{1,3,2,0:T(8,128)(2,1)}, f32[4,3,512,1]{2,1,3,0:T(4,128)}, bf16[4,512,3,3,64]{1,4,3,2,0:T(8,128)(2,1)}, s32[4]{0:T(128)S(1)}, /*index=5*/s32[]{:T(128)}) while((s32[]{:T(128)}, bf16[4,512,3,64]{1,3,2,0:T(8,128)(2,1)}, f32[4,3,512,1]{2,1,3,0:T(4,128)}, bf16[4,512,3,3,64]{1,4,3,2,0:T(8,128)(2,1)}, ...), condition=%wide.region_3.4_spmd, body=%wide.region_0.3_spmd.sunk | while | flops 210074624 | bytes 11459673 | solution.py:123
  81.4 4.2 all-to-all-start.1
  91.3 6.1 all-to-all-done.1
  97.3 2.8 fusion.57
  101.3 20.0 %multiply_convert_fusion.1 = (bf16[512,3072]{1,0:T(8,128)(2,1)S(1)}, f32[512,3072]{1,0:T(8,128)}, f32[512,3072]{1,0:T(8,128)}) fusion(f32[3072]{0:T(1024)S(1)} %copy-done.35, bf16[768,3072]{1,0:T(8,128)(2,1)} %param.25, f32[512,768]{1,0:T(8,128)S(1)} %get-tuple-element.169, f32[768]{0:T(1024)S(1)} %copy-done.31, f32[768]{0:T(1024)S(1)} %get-tuple-element.180, ...), kind=kOutput, calls=%fused_computation.50 | convolution fusion | flops 2521694208 | bytes 22042624 | tf_op jit(solution)/shard_map/dot_general | solution.py:144
  121.3 2.8 fusion.58
  136.6 3.2 multiply_reduce_fusion.1
  146.1 9.7 %convert_reduce_fusion = (f32[3072]{0:T(1024)}, bf16[512,3072]{1,0:T(8,128)(2,1)S(1)}) fusion(f32[512,3072]{1,0:T(8,128)} %get-tuple-element.156, f32[512,3072]{1,0:T(8,128)} %get-tuple-element.170, f32[3072]{0:T(1024)} %param.31, bf16[512,768]{1,0:T(8,128)(2,1)S(1)} %get-tuple-element.148, bf16[3072,768]{1,0:T(8,128)(2,1)} %param.26), kind=kOutput, calls=%fused_computation.48 | convolution fusion | flops 2442654720 | bytes 21258240 | tf_op jit(solution)/shard_map/dot_general | solution.py:30
  155.8 7.3 multiply_reduce_fusion.2
  170.0 4.2 all-to-all-start.2
  174.3 3.6 fusion.61
  177.9 8.0 %all-to-all-done.2 = bf16[512,4,192]{0,2,1:T(8,128)(2,1)} async-done(((bf16[512,4,192]{0,2,1:T(8,128)(2,1)}), bf16[512,4,192]{0,2,1:T(8,128)(2,1)}, u32[]{:S(2)}, u32[]{:S(2)}) %all-to-all-start.2) | async-done | bytes 786464 | tf_op jit(solution)/shard_map/all_to_all | solution.py:177
  185.9 39.9 %while.24 = (s32[]{:T(128)}, bf16[4,512,3,3,64]{1,4,3,2,0:T(8,128)(2,1)}, bf16[4,512,3,3,64]{1,4,3,2,0:T(8,128)(2,1)}, s32[4]{0:T(128)}, f32[4,3,512,1]{2,1,3,0:...) while((s32[]{:T(128)}, bf16[4,512,3,3,64]{1,4,3,2,0:T(8,128)(2,1)}, ...), condition=%wide.region_16.17_spmd, body=%wide.region_14.16_spmd.sunk | while | flops 512654336 | bytes 27953856 | solution.py:185
  225.8 4.9 copy.60
  230.7 5.9 reshape.350
  236.6 7.0 copy.61
  243.6 54.1 %all_to_all.50 = bf16[2048,3,1,192]{3,1,2,0:T(4,128)(2,1)} all-to-all(bf16[2048,3,1,192]{3,1,2,0:T(4,128)(2,1)} %copy.61), channel_id=1, replica_groups=mesh['batch'=8,'head'=4] {'head'}, dimensions={0} | all-to-all | bytes 4718592 | tf_op jit(solution)/shard_map/all_to_all | solution.py:186
  297.6 7.4 copy.70
  308.7 5.0 convolution_bitcast_fusion
  313.7 8.8 %fusion.48 = f32[768,3072]{0,1:T(8,128)} fusion(bf16[512,3072]{1,0:T(8,128)(2,1)} %copy-done.41, f32[512,768]{1,0:T(8,128)} %copy-done.6, f32[768]{0:T(1024)} %get-tuple-element.107, f32[768]{0:T(1024)S(1)} %copy-done.26, f32[512]{0:T(512)} %copy-done.27, f32[512]{0:T(512)S(1)} %copy-done.16), kind=kOutput, calls=%fused_computation.139 | convolution fusion | flops 2417885184 | bytes 14166016 | tf_op jit(solution)/shard_map/dot_general | solution.py:24
  322.6 8.4 %fusion.62 = f32[3072,768]{0,1:T(8,128)} fusion(bf16[512,3072]{1,0:T(8,128)(2,1)} %copy-done.40, bf16[512,768]{1,0:T(8,128)(2,1)} %copy-done.12), kind=kOutput, calls=%fused_computation.150 | convolution fusion | flops 2415919104 | bytes 13369344 | tf_op jit(solution)/shard_map/dot_general | solution.py:24
  338.6 2.7 convert_reduce_fusion.1
  349.2 42.6 %all-reduce.5 = (f32[3,768]{1,0:T(4,128)}, f32[6,768]{1,0:T(8,128)}, f32[2,768]{1,0:T(2,128)}, f32[3072]{0:T(1024)}, f32[768]{0:T(1024)}) all-reduce(f32[3,768]{1,0:T(4,128)S(1)} %broadcast_multiply_fusion.1, f32[6,768]{1,0:T(8,128)} %stack.58, ...), channel_id=7, replica_groups=mesh['batch'=8,'head'=4] {'batch','head'}, use_global_device_ids=true, to_apply=%region_24.25.clone | all-reduce | flops 12288 | bytes 98304
  398.4 5.1 add_convert_fusion.1
  403.5 70.7 %reduce-scatter.9.cloned.1.call-done = f32[768,72]{0,1:T(8,128)} async-done(((f32[768,2304]{0,1:T(8,128)}), f32[768,72]{0,1:T(8,128)}) %reduce-scatter.9.cloned.1.call-update) | async-done | bytes 221200 | tf_op jit(solution)/shard_map/reduce_scatter | solution.py:202
  474.2 142.0 %reduce-scatter.13.cloned.1.call-done = f32[768,96]{0,1:T(8,128)} async-done(((f32[768,3072]{0,1:T(8,128)}), f32[768,96]{0,1:T(8,128)}) %reduce-scatter.13.cloned.1.call-update) | async-done | bytes 294928 | tf_op jit(solution)/shard_map/reduce_scatter | solution.py:204
  616.2 141.1 %reduce-scatter.15.cloned.1.call-done = f32[3072,24]{0,1:T(8,128)} async-done(((f32[3072,768]{0,1:T(8,128)}), f32[3072,24]{0,1:T(8,128)}) %reduce-scatter.15.cloned.1.call-update) | async-done | bytes 294928 | tf_op jit(solution)/shard_map/reduce_scatter | solution.py:205
  (242 shorter events, 123.5 us)
Async XLA Ops:
  8.8 112.4 %copy-start.25 = (f32[768]{0:T(1024)}, f32[768]{0:T(1024)S(1)}, u32[]{:S(2)}) copy-start(f32[768]{0:T(1024)S(1)} %get-tuple-element.180) | copy-start | bytes 9220
  21.3 33.8 %copy-start.38 = (s32[4]{0:T(128)S(1)}, s32[4]{0:T(128)}, u32[]{:S(2)}) copy-start(s32[4]{0:T(128)} %param.21) | copy-start | bytes 52
  21.3 33.8 %all-to-all-start = ((bf16[512,3,4,192]{0,3,1,2:T(8,128)(2,1)}), bf16[512,3,4,192]{0,3,1,2:T(8,128)(2,1)}, u32[]{:S(2)}, u32[]{:S(2)}) async-start(bf16[512,3,4,192]{0,3,1,2:T(8,128)(2,1)} %copy.58), calls=%async_computation | async-start | bytes 4718592 | tf_op jit(solution)/shard_map/all_to_all | solution.py:115
  79.1 7.8 %copy-start.37 = (s32[4]{0:T(128)S(1)}, s32[4]{0:T(128)}, u32[]{:S(2)}) copy-start(s32[4]{0:T(128)} %param.22) | copy-start | bytes 52
  81.4 15.9 %all-to-all-start.1 = ((bf16[4,512,1,192]{1,3,2,0:T(8,128)(2,1)}), bf16[4,512,1,192]{1,3,2,0:T(8,128)(2,1)}, u32[]{:S(2)}, u32[]{:S(2)}) async-start(bf16[4,512,1,192]{1,3,2,0:T(8,128)(2,1)} %pad_maximum_fusion), calls=%async_computation.1 | async-start | bytes 1572864 | tf_op jit(solution)/shard_map/all_to_all | solution.py:125
  85.6 317.9 %reduce-scatter.17.cloned.1.call-start = ((), (), s32[]{:S(2)}) async-start(), calls=%async_computation.13 | async-start | bytes 2433024 | tf_op jit(solution)/shard_map/reduce_scatter | solution.py:206
  97.3 3.9 copy-start.31
  97.3 3.9 copy-start.35
  97.3 24.0 %slice-start = ((s8[4718592]{0:T(1024)(128)(4,1)}), s8[4194304]{0:T(1024)(128)(4,1)S(1)}, s32[]{:S(2)}) async-start(s8[4718592]{0:T(1024)(128)(4,1)} %bitcast.204), calls=%async_computation.14 | async-start | bytes 8388608
  100.2 21.1 %copy-start.6 = (f32[512,768]{1,0:T(8,128)}, f32[512,768]{1,0:T(8,128)S(1)}, u32[]{:S(2)}) copy-start(f32[512,768]{1,0:T(8,128)S(1)} %get-tuple-element.169) | copy-start | bytes 4718596
  100.2 21.1 %copy-start.15 = (f32[512]{0:T(512)}, f32[512]{0:T(512)S(1)}, u32[]{:S(2)}) copy-start(f32[512]{0:T(512)S(1)} %broadcast_multiply_fusion.3) | copy-start | bytes 6148
  101.3 20.0 %copy-start.27 = (f32[512]{0:T(512)}, f32[512]{0:T(512)S(1)}, u32[]{:S(2)}) copy-start(f32[512]{0:T(512)S(1)} %fusion.43) | copy-start | bytes 6148
  101.3 20.0 %copy-start.32 = (f32[768]{0:T(1024)S(1)}, f32[768]{0:T(1024)}, u32[]{:S(2)}) copy-start(f32[768]{0:T(1024)} %get-tuple-element.106) | copy-start | bytes 9220
  101.3 20.0 %slice-start.1 = ((s8[4718592]{0:T(1024)(128)(4,1)}), s8[524288]{0:T(1024)(128)(4,1)S(1)}, s32[]{:S(2)}) async-start(s8[4718592]{0:T(1024)(128)(4,1)} %bitcast.204), calls=%async_computation.15 | async-start | bytes 1048576
  124.1 10.5 %copy-start.1 = (f32[512,768]{1,0:T(8,128)}, f32[512,768]{1,0:T(8,128)S(1)}, u32[]{:S(2)}) copy-start(f32[512,768]{1,0:T(8,128)S(1)} %get-tuple-element.172) | copy-start | bytes 4718596
  124.2 10.5 %copy-start.24 = (f32[768]{0:T(1024)S(1)}, f32[768]{0:T(1024)}, u32[]{:S(2)}) copy-start(f32[768]{0:T(1024)} %slice_reduce_fusion) | copy-start | bytes 9220
  136.6 3.9 copy-start.2
  136.6 3.9 copy-start.4
  146.0 9.7 %copy-start.12 = (bf16[512,768]{1,0:T(8,128)(2,1)}, bf16[512,768]{1,0:T(8,128)(2,1)S(1)}, u32[]{:S(2)}) copy-start(bf16[512,768]{1,0:T(8,128)(2,1)S(1)} %get-tuple-element.148) | copy-start | bytes 2359300
  146.0 9.7 %copy-start.7 = (f32[512,768]{1,0:T(8,128)S(1)}, f32[512,768]{1,0:T(8,128)}, u32[]{:S(2)}) copy-start(f32[512,768]{1,0:T(8,128)} %copy-done.6) | copy-start | bytes 4718596
  146.0 9.7 %copy-start.9 = (f32[512,768]{1,0:T(8,128)S(1)}, f32[512,768]{1,0:T(8,128)}, u32[]{:S(2)}) copy-start(f32[512,768]{1,0:T(8,128)} %get-tuple-element.154) | copy-start | bytes 4718596
  146.1 9.7 %copy-start.16 = (f32[512]{0:T(512)S(1)}, f32[512]{0:T(512)}, u32[]{:S(2)}) copy-start(f32[512]{0:T(512)} %copy-done.15) | copy-start | bytes 6148
  146.1 9.7 %copy-start.26 = (f32[768]{0:T(1024)S(1)}, f32[768]{0:T(1024)}, u32[]{:S(2)}) copy-start(f32[768]{0:T(1024)} %copy-done.25) | copy-start | bytes 9220
  146.1 9.7 %copy-start.28 = (f32[512]{0:T(512)S(1)}, f32[512]{0:T(512)}, u32[]{:S(2)}) copy-start(f32[512]{0:T(512)} %copy-done.27) | copy-start | bytes 6148
  155.8 7.3 copy-start.41
  155.8 7.3 copy-start.18
  170.0 15.9 %all-to-all-start.2 = ((bf16[512,4,192]{0,2,1:T(8,128)(2,1)}), bf16[512,4,192]{0,2,1:T(8,128)(2,1)}, u32[]{:S(2)}, u32[]{:S(2)}) async-start(bf16[512,4,192]{0,2,1:T(8,128)(2,1)} %bitcast.199), calls=%async_computation.2 | async-start | bytes 1572864 | tf_op jit(solution)/shard_map/all_to_all | solution.py:177
  174.2 229.3 %reduce-scatter.11.cloned.1.call-start = ((), (), s32[]{:S(2)}) async-start(), calls=%async_computation.10 | async-start | bytes 2433024 | tf_op jit(solution)/shard_map/reduce_scatter | solution.py:203
  177.9 296.3 %reduce-scatter.9.cloned.1.call-start = ((), (), s32[]{:S(2)}) async-start(), calls=%async_computation.9 | async-start | bytes 7299072 | tf_op jit(solution)/shard_map/reduce_scatter | solution.py:202
  313.7 302.5 %reduce-scatter.13.cloned.1.call-start = ((), (), s32[]{:S(2)}) async-start(), calls=%async_computation.11 | async-start | bytes 9732096 | tf_op jit(solution)/shard_map/reduce_scatter | solution.py:204
  322.5 434.8 %reduce-scatter.15.cloned.1.call-start = ((), (), s32[]{:S(2)}) async-start(), calls=%async_computation.12 | async-start | bytes 9732096 | tf_op jit(solution)/shard_map/reduce_scatter | solution.py:205
  331.6 17.6 %copy-start.23 = (f32[768]{0:T(1024)S(1)}, f32[768]{0:T(1024)}, u32[]{:S(2)}) copy-start(f32[768]{0:T(1024)} %get-tuple-element.176) | copy-start | bytes 9220
  (23 other events, 52.6 us)
Sparse Core Ops, SparseCore 0:
  144.5 100.3 reduce-scatter.16
  251.7 98.0 reduce-scatter.10
  356.0 118.0 reduce-scatter.8
  481.5 134.6 reduce-scatter.12
  622.5 134.7 reduce-scatter.14
